TPU v7x, 512 devices: a whole 4x4x16 slice. The times are simulated.
512 devices in a mesh: row: 128 (over y, z, core), col: 4 (over x).
Axes of the slice: x: 4, y: 4, z: 16, core: 2. Of those that a mesh axis runs over, the one named last changes fastest.
Arguments:
- residual: float32 [65536, 128], P('row'), may hold values from -6 to 6
- solution: float32 [65536, 128], P('row'), may hold values from -6 to 6
- near_field_blocks: float32 [256, 4, 256, 256], P('row', 'col'), may hold values from -0.09375 to 0.09375
- near_cols: int32 [256, 4], P('row', 'col'), may hold values from 0 to 255, as said below
- couplings: float32 [256, 64, 16, 16], P('row', 'col'), may hold values from -0.1875 to 0.1875
- far_cols: int32 [256, 64], P('row', 'col'), may hold values from 0 to 255, as said below
- far_count: int32 [256], P('row'), may hold values from 16 to 64, as said below
- col_basis: float32 [256, 16, 256], P('row'), may hold values from -0.375 to 0.375
- row_basis: float32 [256, 16, 256], P('row'), may hold values from -0.75 to 0.75
Outputs:
- solution_next: float32 [65536, 128], P('row')
- hessenberg: float32 [5, 4, 128], replicated
Inputs may be any that keep to these rules, and one draw needn't show every extreme that they name: near_cols[i, 0] = i; the other entries of row cluster i are i + t for distinct nonzero t with |t| <= 2, clipped to 0 .. 255. far_cols[i, p] differs from i by more than 2, counted around the ends of the cluster range. Slots p >= far_count[i] of row cluster i are unused; some row cluster uses all 64 slots.
All inputs are finite; a program needn't handle non-finite values.
Results may differ from a plain program's by a relative error of at most 0.0001.
Values sent between devices are 32-bit elements; how exact they have to be, the bound alone decides.
A program may use at most 64 MiB of HBM per device.

v0:
```python
import jax
import jax.numpy as jnp
from jax import lax
from jax.sharding import PartitionSpec as P

LEAF_UNKNOWNS = 256
CL_DEV = 2
REACH = 2
SB = 4
HIGH = lax.Precision.HIGHEST
SHIFT = 1.0


def with_halo(value, sides, width):
    for axis, dim in sides:
        peers, length = (lax.axis_size(axis), value.shape[dim])
        up = [(i, (i + 1) % peers) for i in range(peers - 1)]
        down = [(j, i) for i, j in up]
        last = lax.slice_in_dim(value, length - width, length, axis=dim)
        first = lax.slice_in_dim(value, 0, width, axis=dim)
        before = lax.ppermute(last, axis, up)
        after = lax.ppermute(first, axis, down)
        value = jnp.concatenate([before, value, after], axis=dim)
    return value


def cholesky_upper(entries, order_n):
    zero_entry = jnp.zeros_like(entries[0][0])
    upper_r = []
    for row_idx in range(order_n):
        upper_r.append([zero_entry] * order_n)
    for row_idx in range(order_n):
        running = entries[row_idx][row_idx]
        for earlier in range(row_idx):
            running = running - upper_r[earlier][row_idx] * upper_r[earlier][row_idx]
        pivot_val = jnp.sqrt(running)
        upper_r[row_idx][row_idx] = pivot_val
        for col_idx in range(row_idx + 1, order_n):
            entry_val = entries[row_idx][col_idx]
            for earlier in range(row_idx):
                entry_val = entry_val - upper_r[earlier][row_idx] * upper_r[earlier][col_idx]
            upper_r[row_idx][col_idx] = entry_val / pivot_val
    return upper_r


def small_update(gram_sum, scale_factor, depth_n):
    order_n = depth_n + 1
    entries = [
        [gram_sum[row_idx, col_idx] for col_idx in range(order_n)] for row_idx in range(order_n)
    ]
    upper_r = cholesky_upper(entries, order_n)
    shifted = [
        [
            SHIFT * upper_r[row_idx][col_idx] + upper_r[row_idx][col_idx + 1]
            for col_idx in range(depth_n)
        ]
        for row_idx in range(order_n)
    ]
    hessen = []
    for row_idx in range(order_n):
        row_vals = []
        for col_idx in range(depth_n):
            entry_val = shifted[row_idx][col_idx]
            for earlier in range(col_idx):
                entry_val = entry_val - row_vals[earlier] * upper_r[earlier][col_idx]
            row_vals.append(entry_val / upper_r[col_idx][col_idx])
        hessen.append(row_vals)
    normal = []
    for row_idx in range(depth_n):
        row_vals = []
        for col_idx in range(depth_n):
            entry_val = hessen[0][row_idx] * hessen[0][col_idx]
            for inner in range(1, order_n):
                entry_val = entry_val + hessen[inner][row_idx] * hessen[inner][col_idx]
            row_vals.append(entry_val)
        normal.append(row_vals)
    target = [scale_factor * upper_r[0][0] * hessen[0][col_idx] for col_idx in range(depth_n)]
    factor = cholesky_upper(normal, depth_n)
    forward = []
    for row_idx in range(depth_n):
        entry_val = target[row_idx]
        for earlier in range(row_idx):
            entry_val = entry_val - factor[earlier][row_idx] * forward[earlier]
        forward.append(entry_val / factor[row_idx][row_idx])
    solved = [None] * depth_n
    for row_idx in range(depth_n - 1, -1, -1):
        entry_val = forward[row_idx]
        for later in range(row_idx + 1, depth_n):
            entry_val = entry_val - factor[row_idx][later] * solved[later]
        solved[row_idx] = entry_val / factor[row_idx][row_idx]
    weights = [None] * depth_n
    for row_idx in range(depth_n - 1, -1, -1):
        entry_val = solved[row_idx]
        for later in range(row_idx + 1, depth_n):
            entry_val = entry_val - upper_r[row_idx][later] * weights[later]
        weights[row_idx] = entry_val / upper_r[row_idx][row_idx]
    hess_array = jnp.stack([jnp.stack(hessen[row_idx], 0) for row_idx in range(order_n)], 0)
    return (hess_array, weights)


def local(
    residual,
    solution,
    near_field_blocks,
    near_cols,
    couplings,
    far_cols,
    far_count,
    col_basis,
    row_basis,
):
    first_cluster = lax.axis_index("row") * CL_DEV
    blocks, couple = (near_field_blocks, couplings)
    near_idx, far_idx = (near_cols, far_cols)
    positions = lax.axis_index("col") * couplings.shape[1] + jnp.arange(
        couplings.shape[1], dtype=jnp.int32
    )
    live_mask = (positions[None, :] < far_count[:, None]).astype(jnp.float32)
    weighted = couple * live_mask[:, :, None, None]
    local_near = near_idx - (first_cluster - REACH)
    scale_factor = jnp.ones((residual.shape[1],), jnp.float32)
    current = residual
    basis_list = [current]
    for step_k in range(SB):
        width_r = current.shape[1]
        extended = with_halo(current, (("row", 0),), REACH * LEAF_UNKNOWNS)
        panels = extended.reshape(CL_DEV + 2 * REACH, LEAF_UNKNOWNS, width_r)
        picked = jnp.take(panels, local_near, axis=0)
        near_part = jnp.einsum("csab,csbr->car", blocks, picked, precision=HIGH)
        own_panels = current.reshape(CL_DEV, LEAF_UNKNOWNS, width_r)
        coeffs = jnp.einsum("ckb,cbr->ckr", col_basis, own_panels, precision=HIGH)
        table = lax.all_gather(coeffs, "row", axis=0, tiled=True)
        fetched = jnp.take(table, far_idx, axis=0)
        summed = jnp.einsum("cfkl,cflr->ckr", weighted, fetched, precision=HIGH)
        far_part = jnp.einsum("ckb,ckr->cbr", row_basis, summed, precision=HIGH)
        partial_value = (near_part + far_part).reshape(CL_DEV * LEAF_UNKNOWNS, width_r)
        current = lax.psum(partial_value, "col")
        basis_list.append(current)
    stacked = jnp.stack(basis_list, 0)
    local_gram = jnp.einsum("anr,bnr->abr", stacked, stacked, precision=HIGH)
    gram_sum = lax.psum(local_gram, "row")
    hessenberg, weights = small_update(gram_sum, scale_factor, SB)
    new_sol = solution
    for step_k in range(SB):
        new_sol = new_sol + weights[step_k][None, :] * basis_list[step_k]
    return (new_sol, hessenberg)


def solution(mesh):
    placed = (
        P("row", None),
        P("row", None),
        P("row", "col", None, None),
        P("row", "col"),
        P("row", "col", None, None),
        P("row", "col"),
        P("row"),
        P("row", None, None),
        P("row", None, None),
    )
    return jax.shard_map(
        local, mesh=mesh, in_specs=placed, out_specs=(P("row", None), P()), check_vma=False
    )
```

profile of v0, /device:TPU:4, one launch (start us, length us, event | category | flops | bytes accessed | tf_op | source)
XLA Modules:
  0.0 1346.1 jit_solution(8567163214037070050)
XLA Ops:
  7.2 1.9 fusion.85
  9.2 1.8 collective-permute-start
  11.0 1.3 collective-permute-start.1
  12.3 0.7 compare_select_fusion
  13.1 0.7 and_bitcast_fusion
  13.7 0.8 compare_and_fusion
  14.5 1.8 collective-permute-done.1
  16.3 1.0 pad_maximum_fusion
  17.9 139.1 %all-gather.5.cloned.1.call-done = f32[256,16,128]{2,1,0:T(8,128)} async-done(((f32[2,16,128]{2,1,0:T(8,128)}), f32[256,16,128]{2,1,0:T(8,128)}) %all-gather.5.cloned.1.call-update) | async-done | bytes 2097168 | tf_op jit(solution)/shard_map/all_gather | solution.py:132
  157.0 2.2 gather_fusion.1
  159.2 0.8 convolution_bitcast_fusion.7
  160.4 0.8 fusion.3
  161.3 0.8 copy.47
  162.2 52.8 %all-reduce.5.cloned.1.call-done = f32[512,128]{0,1:T(8,128)} async-done(((f32[512,128]{0,1:T(8,128)}), f32[512,128]{0,1:T(8,128)}) %all-reduce.5.cloned.1.call-update) | async-done | bytes 262160 | tf_op jit(solution)/shard_map/psum | solution.py:137
  215.1 1.1 copy.50
  216.1 0.9 convolution_bitcast_fusion.3
  217.1 1.3 collective-permute-start.2
  218.4 1.3 collective-permute-start.3
  219.7 4.1 collective-permute-done.3
  223.8 1.0 pad_maximum_fusion.1
  225.1 0.6 gather_fusion.2
  225.7 135.3 %all-gather.7.cloned.1.call-done = f32[256,16,128]{2,1,0:T(8,128)} async-done(((f32[2,16,128]{2,1,0:T(8,128)}), f32[256,16,128]{2,1,0:T(8,128)}) %all-gather.7.cloned.1.call-update) | async-done | bytes 2097168 | tf_op jit(solution)/shard_map/all_gather | solution.py:132
  360.9 2.2 gather_fusion.3
  363.1 0.8 convolution_bitcast_fusion.6
  364.3 0.8 fusion.2
  365.2 0.8 copy.52
  366.2 52.8 %all-reduce.7.cloned.1.call-done = f32[512,128]{0,1:T(8,128)} async-done(((f32[512,128]{0,1:T(8,128)}), f32[512,128]{0,1:T(8,128)}) %all-reduce.7.cloned.1.call-update) | async-done | bytes 262160 | tf_op jit(solution)/shard_map/psum | solution.py:137
  419.0 1.1 copy.55
  420.0 0.9 convolution_bitcast_fusion.2
  421.0 1.3 collective-permute-start.4
  422.3 1.3 collective-permute-start.5
  423.6 4.1 collective-permute-done.5
  427.7 1.0 pad_maximum_fusion.2
  429.0 0.6 gather_fusion.4
  429.6 135.1 %all-gather.9.cloned.1.call-done = f32[256,16,128]{2,1,0:T(8,128)} async-done(((f32[2,16,128]{2,1,0:T(8,128)}), f32[256,16,128]{2,1,0:T(8,128)}) %all-gather.9.cloned.1.call-update) | async-done | bytes 2097168 | tf_op jit(solution)/shard_map/all_gather | solution.py:132
  564.7 2.2 gather_fusion.5
  566.8 0.8 convolution_bitcast_fusion.5
  568.1 0.8 fusion.1
  569.0 0.8 copy.57
  569.9 52.8 %all-reduce.9.cloned.1.call-done = f32[512,128]{0,1:T(8,128)} async-done(((f32[512,128]{0,1:T(8,128)}), f32[512,128]{0,1:T(8,128)}) %all-reduce.9.cloned.1.call-update) | async-done | bytes 262160 | tf_op jit(solution)/shard_map/psum | solution.py:137
  622.7 1.1 copy.60
  623.8 0.9 convolution_bitcast_fusion.1
  624.8 1.3 collective-permute-start.6
  626.1 1.5 collective-permute-start.7
  627.6 3.9 collective-permute-done.7
  631.5 1.0 pad_maximum_fusion.3
  633.4 135.3 %all-gather.11.cloned.1.call-done = f32[256,16,128]{2,1,0:T(8,128)} async-done(((f32[2,16,128]{2,1,0:T(8,128)}), f32[256,16,128]{2,1,0:T(8,128)}) %all-gather.11.cloned.1.call-update) | async-done | bytes 2097168 | tf_op jit(solution)/shard_map/all_gather | solution.py:132
  768.6 2.2 gather_fusion.7
  770.8 0.8 convolution_bitcast_fusion.4
  772.0 0.8 fusion
  772.9 0.8 copy.62
  773.8 0.8 copy.65
  774.6 0.8 copy.76
  775.5 0.8 copy.66
  776.3 1.0 copy.63
  777.3 1.0 copy.64
  778.3 0.9 stack.74
  779.2 47.4 %all-reduce.11.cloned.1.call-done = f32[1,512,128]{1,0,2:T(1,128)} async-done(((f32[1,512,128]{1,0,2:T(1,128)}), f32[1,512,128]{1,0,2:T(1,128)}) %all-reduce.11.cloned.1.call-update) | async-done | bytes 262160 | tf_op jit(solution)/shard_map/psum | solution.py:137
  826.6 4.6 stack.76
  831.2 3.7 convolution_bitcast_fusion
  834.9 495.3 %psum.39 = f32[5,5,128]{0,1,2:T(8,128)S(1)} all-reduce(f32[5,5,128]{0,1,2:T(8,128)} %convolution_bitcast_fusion), channel_id=1, replica_groups=mesh['row'=128,'col'=4] {'row'}, use_global_device_ids=true, to_apply=%region_4.7 | all-reduce | flops 3200 | bytes 25600 | tf_op jit(solution)/shard_map/psum | solution.py:141
  1330.2 6.9 multiply_reduce_fusion
  1337.7 0.8 copy.67
  1338.6 0.6 copy-done.11
  (75 shorter events, 5.4 us)
Async XLA Ops:
  7.2 153.2 %copy-start = (f32[2,1,256,256]{3,2,1,0:T(8,128)S(1)}, f32[2,1,256,256]{3,2,1,0:T(8,128)}, u32[]{:S(2)}) copy-start(f32[2,1,256,256]{3,2,1,0:T(8,128)} %param.15) | copy-start | bytes 1572868
  7.2 152.0 %copy-start.1 = (f32[2,16,16,16]{3,2,1,0:T(8,128)S(1)}, f32[2,16,16,16]{3,2,1,0:T(8,128)}, u32[]{:S(2)}) copy-start(f32[2,16,16,16]{3,2,1,0:T(8,128)} %param.17) | copy-start | bytes 98308
  7.2 152.7 %copy-start.9 = (f32[2,16,256]{2,1,0:T(8,128)S(1)}, f32[2,16,256]{2,1,0:T(8,128)}, u32[]{:S(2)}) copy-start(f32[2,16,256]{2,1,0:T(8,128)} %param.21) | copy-start | bytes 98308
  7.2 149.8 %all-gather.5.cloned.1.call-start = ((), (), s32[]{:S(2)}) async-start(), calls=%async_computation | async-start | bytes 2113536 | tf_op jit(solution)/shard_map/all_gather | solution.py:132
  9.2 205.9 %all-reduce.5.cloned.1.call-start = ((), (), s32[]{:S(2)}) async-start(), calls=%async_computation.1 | async-start | bytes 524288 | tf_op jit(solution)/shard_map/psum | solution.py:137
  9.2 5.3 collective-permute-start
  11.0 5.3 collective-permute-start.1
  159.1 57.0 %copy-start.8 = (f32[2,16,256]{2,1,0:T(8,128)S(1)}, f32[2,16,256]{2,1,0:T(8,128)}, u32[]{:S(2)}) copy-start(f32[2,16,256]{2,1,0:T(8,128)} %param.20) | copy-start | bytes 98308
  162.2 198.8 %all-gather.7.cloned.1.call-start = ((), (), s32[]{:S(2)}) async-start(), calls=%async_computation.2 | async-start | bytes 2113536 | tf_op jit(solution)/shard_map/all_gather | solution.py:132
  217.0 201.9 %all-reduce.7.cloned.1.call-start = ((), (), s32[]{:S(2)}) async-start(), calls=%async_computation.3 | async-start | bytes 524288 | tf_op jit(solution)/shard_map/psum | solution.py:137
  217.1 2.7 collective-permute-start.2
  218.4 5.4 collective-permute-start.3
  366.1 198.6 %all-gather.9.cloned.1.call-start = ((), (), s32[]{:S(2)}) async-start(), calls=%async_computation.4 | async-start | bytes 2113536 | tf_op jit(solution)/shard_map/all_gather | solution.py:132
  420.9 201.8 %all-reduce.9.cloned.1.call-start = ((), (), s32[]{:S(2)}) async-start(), calls=%async_computation.5 | async-start | bytes 524288 | tf_op jit(solution)/shard_map/psum | solution.py:137
  421.0 2.7 collective-permute-start.4
  422.3 5.4 collective-permute-start.5
  569.9 198.7 %all-gather.11.cloned.1.call-start = ((), (), s32[]{:S(2)}) async-start(), calls=%async_computation.6 | async-start | bytes 2113536 | tf_op jit(solution)/shard_map/all_gather | solution.py:132
  624.7 201.9 %all-reduce.11.cloned.1.call-start = ((), (), s32[]{:S(2)}) async-start(), calls=%async_computation.7 | async-start | bytes 524288 | tf_op jit(solution)/shard_map/psum | solution.py:137
  624.8 2.8 collective-permute-start.6
  626.1 5.4 collective-permute-start.7
  633.3 140.5 %copy-start.2 = (f32[512,128]{1,0:T(8,128)S(1)}, f32[512,128]{1,0:T(8,128)}, u32[]{:S(2)}) copy-start(f32[512,128]{1,0:T(8,128)} %param.13) | copy-start | bytes 786436
  771.6 3.9 copy-start.10
  772.0 4.3 copy-start.3
  772.0 5.3 copy-start.4
  772.8 5.5 copy-start.5
  834.9 502.6 %copy-start.6 = (f32[512,128]{0,1:T(8,128)S(1)}, f32[512,128]{0,1:T(8,128)}, u32[]{:S(2)}) copy-start(f32[512,128]{0,1:T(8,128)} %copy.65) | copy-start | bytes 786436
  834.9 502.6 %copy-start.7 = (f32[512,128]{0,1:T(8,128)S(1)}, f32[512,128]{0,1:T(8,128)}, u32[]{:S(2)}) copy-start(f32[512,128]{0,1:T(8,128)} %copy.66) | copy-start | bytes 786436
  1338.6 0.6 copy-start.11
Sparse Core Ops, SparseCore 0:
  11.7 145.1 all-gather.4
  162.3 52.7 all-reduce.4
  218.8 142.1 all-gather.6
  366.2 52.6 all-reduce.6
  422.5 142.1 all-gather.8
  570.0 52.7 all-reduce.8
  626.5 142.1 all-gather.10
  773.9 52.6 all-reduce.10
where the time goes:
time: 1350 us
  waiting for transfers between devices  765 us (57%)
  blocking collectives  495 us (37%)
  local copies, waits for them, and re-layouts  30.2 us (2%)
  matrix products  16.2 us (1%)
  between operations  14.7 us (1%)
  other arithmetic  13.6 us (1%)
    all_gather x4, waiting for transfers between devices, local(): table = lax.all_gather(coeffs, 'row', axis=0, tiled=True)  545 us
    psum x1, blocking collectives, local(): gram_sum = lax.psum(local_gram, 'row')  495 us
    psum x4, waiting for transfers between devices, local(): current = lax.psum(partial_value, 'col')  206 us
  transfers between devices with their start and end apart: 16, of which 12 were waited for; matrix products, arithmetic and copies ran while one was open for 1% of the time, Pallas kernels for 0%

commit v1 on v0

--- a/solution.py
+++ b/solution.py
@@ -9,6 +9,11 @@
 SB = 4
 HIGH = lax.Precision.HIGHEST
 SHIFT = 1.0
+
+
+def panel_treat(s0, device_axis):
+    plain = jax.lax.all_gather(s0, axis_name=device_axis).sum(axis=0)
+    return plain
 
 
 def with_halo(value, sides, width):
@@ -138,7 +143,7 @@
         basis_list.append(current)
     stacked = jnp.stack(basis_list, 0)
     local_gram = jnp.einsum("anr,bnr->abr", stacked, stacked, precision=HIGH)
-    gram_sum = lax.psum(local_gram, "row")
+    gram_sum = panel_treat(local_gram, "row")
     hessenberg, weights = small_update(gram_sum, scale_factor, SB)
     new_sol = solution
     for step_k in range(SB):

time: 1350 us -> 993 us (0.74)
  the two profiles are of different devices: /device:TPU:4 before, /device:TPU:1 now
where the time goes in v1:
time: 993 us; the launch traced here: 991 us
  waiting for transfers between devices  887 us (89%)
  starting transfers between devices  34 us (3%)
  local copies, waits for them, and re-layouts  31.6 us (3%)
  matrix products  16.2 us (2%)
  between operations  14.4 us (1%)
    all_gather x4, waiting for transfers between devices, local(): table = lax.all_gather(coeffs, 'row', axis=0, tiled=True)  524 us
    psum x4, waiting for transfers between devices, local(): current = lax.psum(partial_value, 'col')  201 us
    all_gather x1, waiting for transfers between devices, panel_treat(): plain = jax.lax.all_gather(s0, axis_name=device_axis).sum(axis=0)  143 us
    ppermute x4, starting transfers between devices, with_halo(): before = lax.ppermute(last, axis, up)  22.5 us
  transfers between devices with their start and end apart: 17, of which 16 were waited for; matrix products, arithmetic and copies ran while one was open for 1% of the time, Pallas kernels for 0%

profile of v1, /device:TPU:1, one launch (start us, length us, event | category | flops | bytes accessed | tf_op | source)
XLA Modules:
  0.0 991.4 jit_solution(2834541090725968151)
XLA Ops:
  7.2 1.9 fusion.121
  9.2 4.9 collective-permute-start
  14.1 5.1 collective-permute-start.1
  19.3 0.7 compare_select_fusion
  20.1 0.7 and_bitcast_fusion
  20.7 0.8 compare_and_fusion
  22.0 1.0 pad_maximum_fusion
  23.6 134.6 %all-gather.7.cloned.1.call-done = f32[256,16,128]{2,1,0:T(8,128)} async-done(((f32[2,16,128]{2,1,0:T(8,128)}), f32[256,16,128]{2,1,0:T(8,128)}) %all-gather.7.cloned.1.call-update) | async-done | bytes 2097168 | tf_op jit(solution)/shard_map/all_gather | solution.py:137
  158.2 2.2 gather_fusion.1
  160.4 0.8 convolution_bitcast_fusion.7
  161.6 0.8 fusion.3
  162.5 0.8 copy.48
  163.4 51.1 %all-reduce.5.cloned.1.call-done = f32[512,128]{0,1:T(8,128)} async-done(((f32[512,128]{0,1:T(8,128)}), f32[512,128]{0,1:T(8,128)}) %all-reduce.5.cloned.1.call-update) | async-done | bytes 262160 | tf_op jit(solution)/shard_map/psum | solution.py:142
  214.6 1.1 copy.51
  215.7 0.9 convolution_bitcast_fusion.3
  216.6 5.9 collective-permute-start.2
  222.5 1.9 collective-permute-start.3
  224.4 1.7 collective-permute-done.2
  226.1 4.3 collective-permute-done.3
  230.4 1.0 pad_maximum_fusion.1
  232.2 129.9 %all-gather.9.cloned.1.call-done = f32[256,16,128]{2,1,0:T(8,128)} async-done(((f32[2,16,128]{2,1,0:T(8,128)}), f32[256,16,128]{2,1,0:T(8,128)}) %all-gather.9.cloned.1.call-update) | async-done | bytes 2097168 | tf_op jit(solution)/shard_map/all_gather | solution.py:137
  362.2 2.2 gather_fusion.3
  364.3 0.8 convolution_bitcast_fusion.6
  365.6 0.8 fusion.2
  366.5 0.8 copy.53
  367.4 51.1 %all-reduce.7.cloned.1.call-done = f32[512,128]{0,1:T(8,128)} async-done(((f32[512,128]{0,1:T(8,128)}), f32[512,128]{0,1:T(8,128)}) %all-reduce.7.cloned.1.call-update) | async-done | bytes 262160 | tf_op jit(solution)/shard_map/psum | solution.py:142
  418.5 1.1 copy.56
  419.6 0.9 convolution_bitcast_fusion.2
  420.5 5.9 collective-permute-start.4
  426.4 1.9 collective-permute-start.5
  428.3 1.7 collective-permute-done.4
  430.0 4.3 collective-permute-done.5
  434.3 1.0 pad_maximum_fusion.2
  436.2 129.8 %all-gather.11.cloned.1.call-done = f32[256,16,128]{2,1,0:T(8,128)} async-done(((f32[2,16,128]{2,1,0:T(8,128)}), f32[256,16,128]{2,1,0:T(8,128)}) %all-gather.11.cloned.1.call-update) | async-done | bytes 2097168 | tf_op jit(solution)/shard_map/all_gather | solution.py:137
  565.9 2.2 gather_fusion.5
  568.1 0.8 convolution_bitcast_fusion.5
  569.3 0.8 fusion.1
  570.2 0.8 copy.58
  571.2 51.1 %all-reduce.9.cloned.1.call-done = f32[512,128]{0,1:T(8,128)} async-done(((f32[512,128]{0,1:T(8,128)}), f32[512,128]{0,1:T(8,128)}) %all-reduce.9.cloned.1.call-update) | async-done | bytes 262160 | tf_op jit(solution)/shard_map/psum | solution.py:142
  622.3 1.1 copy.61
  623.4 0.9 convolution_bitcast_fusion.1
  624.3 5.9 collective-permute-start.6
  630.2 1.9 collective-permute-start.7
  632.1 1.7 collective-permute-done.6
  633.8 4.3 collective-permute-done.7
  638.1 1.0 pad_maximum_fusion.3
  640.0 129.9 %all-gather.13.cloned.1.call-done = f32[256,16,128]{2,1,0:T(8,128)} async-done(((f32[2,16,128]{2,1,0:T(8,128)}), f32[256,16,128]{2,1,0:T(8,128)}) %all-gather.13.cloned.1.call-update) | async-done | bytes 2097168 | tf_op jit(solution)/shard_map/all_gather | solution.py:137
  769.9 2.2 gather_fusion.7
  772.0 0.8 convolution_bitcast_fusion.4
  773.3 0.8 fusion
  774.2 0.8 copy.63
  775.3 0.8 copy.79
  776.1 1.0 copy.64
  777.1 1.0 copy.65
  778.1 0.9 stack.74
  779.0 47.2 %all-reduce.11.cloned.1.call-done = f32[1,512,128]{1,0,2:T(1,128)} async-done(((f32[1,512,128]{1,0,2:T(1,128)}), f32[1,512,128]{1,0,2:T(1,128)}) %all-reduce.11.cloned.1.call-update) | async-done | bytes 262160 | tf_op jit(solution)/shard_map/psum | solution.py:142
  826.2 4.6 stack.76
  830.8 3.7 convolution_bitcast_fusion
  834.5 1.8 copy.66
  836.5 1.1 copy.69
  837.6 143.2 %all-gather.15.cloned.1.call-done = f32[640,5,128]{2,1,0:T(8,128)} async-done(((f32[5,5,128]{2,1,0:T(8,128)}), f32[640,5,128]{2,1,0:T(8,128)}) %all-gather.15.cloned.1.call-update) | async-done | bytes 1638416 | tf_op jit(solution)/shard_map/all_gather | solution.py:15
  980.7 2.0 reduce_sum.9
  983.3 0.8 copy.70
  984.3 0.6 copy-done.9
  (76 shorter events, 7.4 us)
Async XLA Ops:
  7.2 154.4 %copy-start = (f32[2,1,256,256]{3,2,1,0:T(8,128)S(1)}, f32[2,1,256,256]{3,2,1,0:T(8,128)}, u32[]{:S(2)}) copy-start(f32[2,1,256,256]{3,2,1,0:T(8,128)} %param.15) | copy-start | bytes 1572868
  7.2 153.2 %copy-start.1 = (f32[2,16,16,16]{3,2,1,0:T(8,128)S(1)}, f32[2,16,16,16]{3,2,1,0:T(8,128)}, u32[]{:S(2)}) copy-start(f32[2,16,16,16]{3,2,1,0:T(8,128)} %param.17) | copy-start | bytes 98308
  7.2 154.0 %copy-start.8 = (f32[2,16,256]{2,1,0:T(8,128)S(1)}, f32[2,16,256]{2,1,0:T(8,128)}, u32[]{:S(2)}) copy-start(f32[2,16,256]{2,1,0:T(8,128)} %param.21) | copy-start | bytes 98308
  7.2 151.0 %all-gather.7.cloned.1.call-start = ((), (), s32[]{:S(2)}) async-start(), calls=%async_computation | async-start | bytes 2113536 | tf_op jit(solution)/shard_map/all_gather | solution.py:137
  9.2 205.4 %all-reduce.5.cloned.1.call-start = ((), (), s32[]{:S(2)}) async-start(), calls=%async_computation.1 | async-start | bytes 524288 | tf_op jit(solution)/shard_map/psum | solution.py:142
  9.2 12.3 %collective-permute-start = (f32[512,128]{1,0:T(8,128)}, f32[512,128]{1,0:T(8,128)S(1)}, u32[]{:S(2)}, u32[]{:S(2)}) collective-permute-start(f32[512,128]{1,0:T(8,128)} %param.13), channel_id=1, source_target_pairs={{0,4},{4,8},{8,12},{12,16},{16,20},{20,24},{24,28},{28,32},{32,36}... | collective-permute-start | bytes 786440 | tf_op jit(solution)/shard_map/ppermute | solution.py:26
  14.1 7.9 collective-permute-start.1
  160.4 55.3 %copy-start.7 = (f32[2,16,256]{2,1,0:T(8,128)S(1)}, f32[2,16,256]{2,1,0:T(8,128)}, u32[]{:S(2)}) copy-start(f32[2,16,256]{2,1,0:T(8,128)} %param.20) | copy-start | bytes 98308
  163.4 198.8 %all-gather.9.cloned.1.call-start = ((), (), s32[]{:S(2)}) async-start(), calls=%async_computation.2 | async-start | bytes 2113536 | tf_op jit(solution)/shard_map/all_gather | solution.py:137
  216.5 202.0 %all-reduce.7.cloned.1.call-start = ((), (), s32[]{:S(2)}) async-start(), calls=%async_computation.3 | async-start | bytes 524288 | tf_op jit(solution)/shard_map/psum | solution.py:142
  216.6 9.5 collective-permute-start.2
  222.5 7.9 collective-permute-start.3
  367.3 198.6 %all-gather.11.cloned.1.call-start = ((), (), s32[]{:S(2)}) async-start(), calls=%async_computation.4 | async-start | bytes 2113536 | tf_op jit(solution)/shard_map/all_gather | solution.py:137
  420.5 201.8 %all-reduce.9.cloned.1.call-start = ((), (), s32[]{:S(2)}) async-start(), calls=%async_computation.5 | async-start | bytes 524288 | tf_op jit(solution)/shard_map/psum | solution.py:142
  420.5 9.5 collective-permute-start.4
  426.4 7.9 collective-permute-start.5
  571.1 198.8 %all-gather.13.cloned.1.call-start = ((), (), s32[]{:S(2)}) async-start(), calls=%async_computation.6 | async-start | bytes 2113536 | tf_op jit(solution)/shard_map/all_gather | solution.py:137
  624.3 202.0 %all-reduce.11.cloned.1.call-start = ((), (), s32[]{:S(2)}) async-start(), calls=%async_computation.7 | async-start | bytes 524288 | tf_op jit(solution)/shard_map/psum | solution.py:142
  624.3 9.5 collective-permute-start.6
  630.2 7.9 collective-permute-start.7
  639.9 135.3 %copy-start.2 = (f32[512,128]{1,0:T(8,128)S(1)}, f32[512,128]{1,0:T(8,128)}, u32[]{:S(2)}) copy-start(f32[512,128]{1,0:T(8,128)} %param.13) | copy-start | bytes 786436
  772.0 4.1 copy-start.3
  772.8 4.3 copy-start.4
  773.3 4.8 copy-start.5
  775.0 205.7 %all-gather.15.cloned.1.call-start = ((), (), s32[]{:S(2)}) async-start(), calls=%async_computation.8 | async-start | bytes 2641920 | tf_op jit(solution)/shard_map/all_gather | solution.py:15
  836.3 146.8 %copy-start.6 = (f32[512,128]{0,1:T(8,128)S(1)}, f32[512,128]{0,1:T(8,128)}, u32[]{:S(2)}) copy-start(f32[512,128]{0,1:T(8,128)} %all-reduce.9.cloned.1.call-done) | copy-start | bytes 786436
  984.2 0.6 copy-start.9
Sparse Core Ops, SparseCore 0:
  11.7 146.4 all-gather.6
  163.5 51.0 all-reduce.4
  218.3 143.8 all-gather.8
  367.5 51.0 all-reduce.6
  422.1 143.8 all-gather.10
  571.2 51.0 all-reduce.8
  626.0 143.8 all-gather.12
  775.2 50.9 all-reduce.10
  836.5 144.2 all-gather.14
